TPU v7x, 32 devices: a whole 2x2x4 slice. The times are simulated.
32 devices in a mesh: groups: 2 (over x), expert: 2 (over core), tensor: 8 (over z, y).
Axes of the slice: x: 2, y: 2, z: 4, core: 2. Of those that a mesh axis runs over, the one named last changes fastest.
Arguments:
- tokens: bfloat16 [2048, 3072], P(('groups', 'expert', 'tensor')), parts along dimension 0, may hold values from -6 to 6
- expert_ids: int32 [2048, 1], P(('groups', 'expert', 'tensor')), parts along dimension 0, may hold values from 0 to 1; in each aligned block of 64 rows (0 to 63, 64 to 127, ...) at most 48 rows name the same one
- gates: float32 [2048], P(('groups', 'expert', 'tensor')), parts along dimension 0, may hold values from 0.2 to 1
- gate_weight: bfloat16 [2, 3072, 16384], P('expert', None, 'tensor'), may hold values from -0.109375 to 0.109375
- up_weight: bfloat16 [2, 3072, 16384], P('expert', None, 'tensor'), may hold values from -0.109375 to 0.109375
- down_weight: bfloat16 [2, 16384, 3072], P('expert', 'tensor'), may hold values from -0.046875 to 0.046875
Outputs:
- routed: bfloat16 [2048, 3072], P(('groups', 'expert', 'tensor')), parts along dimension 0
There are 2 independent parts, one for each index of `groups`. A program takes and returns all parts, laid end to end along the dimension named above; an argument that names none is the same for every part. Nothing has to cross between parts.
Inputs may be any that keep to these rules, and one draw needn't show every extreme that they name: `expert_ids`: among the 64 rows of one device no expert is named more than 48 times; in every draw some device names one expert exactly 48 times.
All inputs are finite; a program needn't handle non-finite values.
Results may differ from a plain program's by a relative error of at most 0.014.
Values may be sent and summed in bfloat16 or wider, within the bound.
A program may use at most 128 MiB of HBM per device.

v0:
```python
import jax
import jax.numpy as jnp
from jax import lax
from jax.sharding import PartitionSpec as P

CAP = 48
IN_CHUNKS = 1
OUT_CHUNKS = 2


def slot_table(expert_ids, experts):
    expert_of = expert_ids[:, 0]
    matches = (expert_of[:, None] == jnp.arange(experts, dtype=jnp.int32)[None, :]).astype(
        jnp.int32
    )
    earlier = jnp.cumsum(matches, axis=0) - matches
    position = jnp.sum(earlier * matches, axis=1)
    column = expert_of * CAP + position
    return (column[:, None] == jnp.arange(experts * CAP, dtype=jnp.int32)[None, :]).astype(
        jnp.bfloat16
    )


def per_device(tokens, expert_ids, gates, gate_weight, up_weight, down_weight):
    rows, width = tokens.shape
    experts = lax.axis_size("expert") * gate_weight.shape[0]
    tensor_size = lax.axis_size("tensor")
    group_ids = lax.all_gather(expert_ids, "tensor", axis=0, tiled=True)
    tables = jax.vmap(slot_table, in_axes=(0, None))(
        group_ids.reshape(tensor_size, rows, 1), experts
    )
    gate_pre, up_pre = (None, None)
    step = width // IN_CHUNKS
    for chunk in range(IN_CHUNKS):
        cut = slice(chunk * step, (chunk + 1) * step)
        gathered = lax.all_gather(tokens[:, cut], "tensor", axis=0)
        outgoing = jnp.einsum("trj,trd->tjd", tables, gathered, preferred_element_type=jnp.float32)
        outgoing = outgoing.astype(jnp.bfloat16).reshape(tensor_size, experts, CAP, step)
        arrived = lax.all_to_all(
            outgoing, "expert", split_axis=1, concat_axis=1, tiled=True
        ).reshape(tensor_size * experts * CAP, step)
        gate_part = jnp.dot(arrived, gate_weight[0, cut], preferred_element_type=jnp.float32)
        up_part = jnp.dot(arrived, up_weight[0, cut], preferred_element_type=jnp.float32)
        gate_pre = gate_part if gate_pre is None else gate_pre + gate_part
        up_pre = up_part if up_pre is None else up_pre + up_part
    hidden = (jax.nn.gelu(gate_pre, approximate=True) * up_pre).astype(jnp.bfloat16)
    step = width // OUT_CHUNKS
    pieces = []
    for chunk in range(OUT_CHUNKS):
        cut = slice(chunk * step, (chunk + 1) * step)
        product = jnp.dot(hidden, down_weight[0, :, cut], preferred_element_type=jnp.float32)
        product = product.astype(jnp.bfloat16).reshape(tensor_size, experts, CAP, step)
        returned = lax.all_to_all(
            product, "expert", split_axis=1, concat_axis=1, tiled=True
        ).reshape(tensor_size, experts * CAP, step)
        placed = jnp.einsum("trj,tjd->trd", tables, returned, preferred_element_type=jnp.float32)
        placed = placed.astype(jnp.bfloat16).reshape(tensor_size * rows, step)
        summed = lax.psum_scatter(placed, "tensor", scatter_dimension=0, tiled=True)
        pieces.append((summed.astype(jnp.float32) * gates[:, None]).astype(jnp.bfloat16))
    return jnp.concatenate(pieces, axis=1) if len(pieces) > 1 else pieces[0]


def solution(mesh):
    return jax.shard_map(
        per_device,
        mesh=mesh,
        in_specs=(
            P(("groups", "expert", "tensor"), None),
            P(("groups", "expert", "tensor"), None),
            P(("groups", "expert", "tensor")),
            P("expert", None, "tensor"),
            P("expert", None, "tensor"),
            P("expert", "tensor", None),
        ),
        out_specs=P(("groups", "expert", "tensor"), None),
        check_vma=False,
    )
```

profile of v0, /device:TPU:0, one launch (start us, length us, event | category | flops | bytes accessed | tf_op | source)
XLA Modules:
  0.0 267.2 jit_solution(1103878211246702654)
XLA Ops:
  6.5 0.7 all-gather.3.cloned.1.call-update
  7.3 0.0 reduce-scatter.5.cloned.1.call-start
  7.3 1.2 dynamic-slice
  9.2 0.8 bitcast_dynamic-update-slice_fusion
  10.0 13.1 %all-reduce = s32[512]{0:T(512)S(1)} all-reduce(s32[512]{0:T(512)S(1)} %bitcast_dynamic-update-slice_fusion), channel_id=1, replica_groups=mesh['groups'=2,'expert'=2,'tensor'=8] {'tensor'}, use_global_device_ids=true, to_apply=%add | all-reduce | flops 512 | bytes 4096
  23.1 0.1 squeeze_reshape.4
  23.1 0.1 copy.26
  23.2 1.4 fusion.33
  24.6 0.1 copy.27
  24.7 47.6 %all-gather.3.cloned.1.call-done = bf16[512,3072]{1,0:T(8,128)(2,1)} async-done(((bf16[64,3072]{1,0:T(8,128)(2,1)}), bf16[512,3072]{1,0:T(8,128)(2,1)}) %all-gather.3.cloned.1.call-update) | async-done | bytes 3145744 | tf_op jit(solution)/shard_map/all_gather | solution.py:36
  72.3 3.4 %convolution_convert_fusion = bf16[8,96,3072]{2,1,0:T(8,128)(2,1)S(1)} fusion(bf16[8,64,3072]{2,1,0:T(8,128)(2,1)} %bitcast.44, s32[8,64]{1,0:T(8,128)S(1)} %multiply_add_fusion), kind=kOutput, calls=%fused_computation.20 | convolution fusion | flops 304398336 | bytes 7866368 | tf_op jit(solution)/shard_map/trj,trd->tjd/dot_general | solution.py:37
  75.7 0.4 copy.28
  76.1 7.9 %all_to_all.15 = bf16[8,2,48,3072]{3,2,0,1:T(8,128)(2,1)S(1)} all-to-all(bf16[8,2,48,3072]{3,2,0,1:T(8,128)(2,1)S(1)} %copy.28), channel_id=1, replica_groups=mesh['groups'=2,'expert'=2,'tensor'=8] {'expert'}, dimensions={1} | all-to-all | bytes 9437184 | tf_op jit(solution)/shard_map/all_to_all | solution.py:39
  84.1 0.4 copy.29
  84.5 1.7 slice-done.2
  86.2 10.0 %fusion.2 = f32[768,2048]{1,0:T(8,128)S(1)} fusion(bf16[768,3072]{1,0:T(8,128)(2,1)S(1)} %bitcast.42, bf16[1,3072,2048]{2,1,0:T(8,128)(2,1)S(1)} %bitcast.48), kind=kOutput, calls=%fused_computation.2 | convolution fusion | flops 9663676416 | bytes 23592960 | tf_op jit(solution)/shard_map/dot_general | solution.py:42
  96.2 14.0 %fusion.12 = bf16[768,2048]{1,0:T(8,128)(2,1)S(1)} fusion(f32[768,2048]{1,0:T(8,128)S(1)} %fusion.2, bf16[768,3072]{1,0:T(8,128)(2,1)S(1)} %bitcast.43, bf16[1,3072,2048]{2,1,0:T(8,128)(2,1)} %param.10), kind=kOutput, calls=%fused_computation.13 | convolution fusion | flops 9679405056 | bytes 26738688 | tf_op jit(solution)/shard_map/dot_general | solution.py:43
  110.3 8.3 %fusion.24 = bf16[768,1536]{1,0:T(8,128)(2,1)S(1)} fusion(bf16[768,2048]{1,0:T(8,128)(2,1)S(1)} %fusion.12, bf16[1,2048,3072]{2,1,0:T(8,128)(2,1)} %param.11), kind=kOutput, calls=%fused_computation.22 | convolution fusion | flops 4833017856 | bytes 11796480 | tf_op jit(solution)/shard_map/dot_general | solution.py:51
  118.6 0.2 copy.32
  118.7 5.6 %all_to_all.16 = bf16[8,2,48,1536]{3,2,0,1:T(8,128)(2,1)S(1)} all-to-all(bf16[8,2,48,1536]{3,2,0,1:T(8,128)(2,1)S(1)} %copy.32), channel_id=1, replica_groups=mesh['groups'=2,'expert'=2,'tensor'=8] {'expert'}, dimensions={1} | all-to-all | bytes 4718592 | tf_op jit(solution)/shard_map/all_to_all | solution.py:53
  124.4 0.2 copy.33
  124.5 1.8 convolution_convert_fusion.1
  126.4 0.0 reduce-scatter.3.cloned.1.call-start
  126.4 8.1 %fusion.21 = bf16[768,1536]{1,0:T(8,128)(2,1)S(1)} fusion(bf16[768,2048]{1,0:T(8,128)(2,1)S(1)} %fusion.12, bf16[1,2048,3072]{2,1,0:T(8,128)(2,1)} %param.11), kind=kOutput, calls=%fused_computation.21 | convolution fusion | flops 4833017856 | bytes 11796480 | tf_op jit(solution)/shard_map/dot_general | solution.py:51
  134.5 0.2 copy.30
  134.7 5.6 %all_to_all.17 = bf16[8,2,48,1536]{3,2,0,1:T(8,128)(2,1)S(1)} all-to-all(bf16[8,2,48,1536]{3,2,0,1:T(8,128)(2,1)S(1)} %copy.30), channel_id=1, replica_groups=mesh['groups'=2,'expert'=2,'tensor'=8] {'expert'}, dimensions={1} | all-to-all | bytes 4718592 | tf_op jit(solution)/shard_map/all_to_all | solution.py:53
  140.3 0.2 copy.31
  140.5 1.8 convolution_convert_fusion.2
  142.3 48.5 %reduce-scatter.5.cloned.1.call-done = bf16[64,1536]{1,0:T(8,128)(2,1)} async-done(((bf16[512,1536]{1,0:T(8,128)(2,1)}), bf16[64,1536]{1,0:T(8,128)(2,1)}) %reduce-scatter.5.cloned.1.call-update) | async-done | bytes 196624 | tf_op jit(solution)/shard_map/reduce_scatter | solution.py:58
  190.8 67.9 %reduce-scatter.3.cloned.1.call-done = bf16[64,1536]{1,0:T(8,128)(2,1)} async-done(((bf16[512,1536]{1,0:T(8,128)(2,1)}), bf16[64,1536]{1,0:T(8,128)(2,1)}) %reduce-scatter.3.cloned.1.call-update) | async-done | bytes 196624 | tf_op jit(solution)/shard_map/reduce_scatter | solution.py:58
  258.7 1.2 multiply_convert_fusion.1
  259.9 0.8 pad_maximum_fusion
  (13 shorter events, 0.1 us)
Async XLA Ops:
  6.5 65.8 %all-gather.3.cloned.1.call-start = ((), (), s32[]{:S(2)}) async-start(), calls=%async_computation.7 | async-start | bytes 3538944 | tf_op jit(solution)/shard_map/all_gather | solution.py:36
  7.3 183.5 %reduce-scatter.5.cloned.1.call-start = ((), (), s32[]{:S(2)}) async-start(), calls=%async_computation.6 | async-start | bytes 1769472 | tf_op jit(solution)/shard_map/reduce_scatter | solution.py:58
  75.7 8.8 %slice-start = ((s8[12582912]{0:T(1024)(128)(4,1)}), s8[4194304]{0:T(1024)(128)(4,1)S(1)}, s32[]{:S(2)}) async-start(s8[12582912]{0:T(1024)(128)(4,1)} %bitcast.47), calls=%async_computation.8 | async-start | bytes 8388608
  76.1 8.4 %slice-start.1 = ((s8[12582912]{0:T(1024)(128)(4,1)}), s8[4194304]{0:T(1024)(128)(4,1)S(1)}, s32[]{:S(2)}) async-start(s8[12582912]{0:T(1024)(128)(4,1)} %bitcast.47), calls=%async_computation.9 | async-start | bytes 8388608
  84.1 2.2 slice-start.2
  126.4 132.3 %reduce-scatter.3.cloned.1.call-start = ((), (), s32[]{:S(2)}) async-start(), calls=%async_computation.5 | async-start | bytes 1769472 | tf_op jit(solution)/shard_map/reduce_scatter | solution.py:58
  140.3 118.4 %copy-start = (f32[64]{0:T(128)S(1)}, f32[64]{0:T(128)}, u32[]{:S(2)}) copy-start(f32[64]{0:T(128)} %param.8) | copy-start | bytes 772
Sparse Core Ops, SparseCore 0:
  9.5 62.7 all-gather.2
  126.5 64.2 reduce-scatter.4
  194.2 64.4 reduce-scatter.2
where the time goes:
time: 268 us; the launch traced here: 267 us
  waiting for transfers between devices  165 us (62%)
  matrix products  47.3 us (18%)
  blocking collectives  32.3 us (12%)
  between operations  13.9 us (5%)
  local copies, waits for them, and re-layouts  5.52 us (2%)
  other arithmetic  3.31 us (1%)
    reduce_scatter x2, waiting for transfers between devices, per_device(): summed = lax.psum_scatter(placed, 'tensor', scatter_dimension=0, tiled=True)  116 us
    all_gather x1, waiting for transfers between devices, per_device(): gathered = lax.all_gather(tokens[:, cut], 'tensor', axis=0)  47.6 us
    dot_general x2, matrix products, per_device(): jnp.dot(hidden, down_weight[0, :, cut], preferred_element_type=jnp.float32)  16.4 us
    dot_general x1, matrix products, per_device(): jnp.dot(arrived, up_weight[0, cut], preferred_element_type=jnp.float32)  14 us
    unnamed x1, blocking collectives  13.1 us
    all_to_all x2, blocking collectives, per_device(): lax.all_to_all(product, 'expert', split_axis=1, concat_axis=1, tiled=True)  11.3 us
    dot_general x1, matrix products, per_device(): jnp.dot(arrived, gate_weight[0, cut], preferred_element_type=jnp.float32)  9.97 us
    all_to_all x1, blocking collectives, per_device(): lax.all_to_all(outgoing, 'expert', split_axis=1, concat_axis=1, tiled=True)  7.92 us
  transfers between devices with their start and end apart: 3, of which 3 were waited for; matrix products, arithmetic and copies ran while one was open for 5% of the time, Pallas kernels for 0%

commit v1 on v0

--- a/solution.py
+++ b/solution.py
@@ -50,8 +50,11 @@
         cut = slice(chunk * step, (chunk + 1) * step)
         product = jnp.dot(hidden, down_weight[0, :, cut], preferred_element_type=jnp.float32)
         product = product.astype(jnp.bfloat16).reshape(tensor_size, experts, CAP, step)
-        returned = lax.all_to_all(
-            product, "expert", split_axis=1, concat_axis=1, tiled=True
+        returned = jnp.concatenate(
+            lax.all_to_all(
+                jnp.stack(jnp.split(product, lax.axis_size("expert"), axis=1)), "expert", 0, 0
+            ),
+            axis=1,
         ).reshape(tensor_size, experts * CAP, step)
         placed = jnp.einsum("trj,tjd->trd", tables, returned, preferred_element_type=jnp.float32)
         placed = placed.astype(jnp.bfloat16).reshape(tensor_size * rows, step)

time: 268 us -> 268 us (level)
  no operation moved by 1% of the time
where the time goes in v1:
time: 268 us; the launch traced here: 267 us
  waiting for transfers between devices  165 us (62%)
  matrix products  47.3 us (18%)
  blocking collectives  32.3 us (12%)
  between operations  13.9 us (5%)
  local copies, waits for them, and re-layouts  5.53 us (2%)
  other arithmetic  3.74 us (1%)
    reduce_scatter x2, waiting for transfers between devices, per_device(): summed = lax.psum_scatter(placed, 'tensor', scatter_dimension=0, tiled=True)  116 us
    all_gather x1, waiting for transfers between devices, per_device(): gathered = lax.all_gather(tokens[:, cut], 'tensor', axis=0)  47.6 us
    dot_general x2, matrix products, per_device(): jnp.dot(hidden, down_weight[0, :, cut], preferred_element_type=jnp.float32)  16.4 us
    dot_general x1, matrix products, per_device(): jnp.dot(arrived, up_weight[0, cut], preferred_element_type=jnp.float32)  14 us
    unnamed x1, blocking collectives  13.1 us
    all_to_all x2, blocking collectives, per_device(): lax.all_to_all(jnp.stack(jnp.split(product, lax.axis_size('expert'), axis...  11.3 us
    dot_general x1, matrix products, per_device(): jnp.dot(arrived, gate_weight[0, cut], preferred_element_type=jnp.float32)  9.97 us
    all_to_all x1, blocking collectives, per_device(): lax.all_to_all(outgoing, 'expert', split_axis=1, concat_axis=1, tiled=True)  7.92 us
  transfers between devices with their start and end apart: 3, of which 3 were waited for; matrix products, arithmetic and copies ran while one was open for 5% of the time, Pallas kernels for 0%

profile of v1, /device:TPU:0, one launch (start us, length us, event | category | flops | bytes accessed | tf_op | source)
XLA Modules:
  0.0 267.4 jit_solution(1313389533321267239)
XLA Ops:
  6.5 0.7 all-gather.3.cloned.1.call-update
  7.3 1.2 dynamic-slice
  9.2 0.8 bitcast_dynamic-update-slice_fusion
  10.0 13.1 %all-reduce = s32[512]{0:T(512)S(1)} all-reduce(s32[512]{0:T(512)S(1)} %bitcast_dynamic-update-slice_fusion), channel_id=1, replica_groups=mesh['groups'=2,'expert'=2,'tensor'=8] {'tensor'}, use_global_device_ids=true, to_apply=%add | all-reduce | flops 512 | bytes 4096
  23.1 0.1 squeeze_reshape.4
  23.1 0.1 copy.34
  23.2 1.4 fusion.33
  24.6 0.1 copy.35
  24.7 47.6 %all-gather.3.cloned.1.call-done = bf16[512,3072]{1,0:T(8,128)(2,1)} async-done(((bf16[64,3072]{1,0:T(8,128)(2,1)}), bf16[512,3072]{1,0:T(8,128)(2,1)}) %all-gather.3.cloned.1.call-update) | async-done | bytes 3145744 | tf_op jit(solution)/shard_map/all_gather | solution.py:36
  72.3 3.4 %convolution_convert_fusion = bf16[8,96,3072]{2,1,0:T(8,128)(2,1)S(1)} fusion(bf16[8,64,3072]{2,1,0:T(8,128)(2,1)} %bitcast.60, s32[8,64]{1,0:T(8,128)S(1)} %multiply_add_fusion), kind=kOutput, calls=%fused_computation.20 | convolution fusion | flops 304398336 | bytes 7866368 | tf_op jit(solution)/shard_map/trj,trd->tjd/dot_general | solution.py:37
  75.7 0.4 copy.36
  76.1 7.9 %all_to_all.15 = bf16[8,2,48,3072]{3,2,0,1:T(8,128)(2,1)S(1)} all-to-all(bf16[8,2,48,3072]{3,2,0,1:T(8,128)(2,1)S(1)} %copy.36), channel_id=1, replica_groups=mesh['groups'=2,'expert'=2,'tensor'=8] {'expert'}, dimensions={1} | all-to-all | bytes 9437184 | tf_op jit(solution)/shard_map/all_to_all | solution.py:39
  84.1 0.4 copy.37
  84.5 1.7 slice-done.2
  86.2 10.0 %fusion.2 = f32[768,2048]{1,0:T(8,128)S(1)} fusion(bf16[768,3072]{1,0:T(8,128)(2,1)S(1)} %bitcast.58, bf16[1,3072,2048]{2,1,0:T(8,128)(2,1)S(1)} %bitcast.64), kind=kOutput, calls=%fused_computation.2 | convolution fusion | flops 9663676416 | bytes 23592960 | tf_op jit(solution)/shard_map/dot_general | solution.py:42
  96.2 14.0 %fusion.12 = bf16[768,2048]{1,0:T(8,128)(2,1)S(1)} fusion(f32[768,2048]{1,0:T(8,128)S(1)} %fusion.2, bf16[768,3072]{1,0:T(8,128)(2,1)S(1)} %bitcast.59, bf16[1,3072,2048]{2,1,0:T(8,128)(2,1)} %param.10), kind=kOutput, calls=%fused_computation.13 | convolution fusion | flops 9679405056 | bytes 26738688 | tf_op jit(solution)/shard_map/dot_general | solution.py:43
  110.3 8.3 %fusion.21 = bf16[768,1536]{1,0:T(8,128)(2,1)S(1)} fusion(bf16[768,2048]{1,0:T(8,128)(2,1)S(1)} %fusion.12, bf16[1,2048,3072]{2,1,0:T(8,128)(2,1)} %param.11), kind=kOutput, calls=%fused_computation.21 | convolution fusion | flops 4833017856 | bytes 11796480 | tf_op jit(solution)/shard_map/dot_general | solution.py:51
  118.6 0.2 slice_bitcast_fusion.3
  118.7 0.2 pad_maximum_fusion
  119.0 5.6 %all_to_all.16 = bf16[2,8,1,48,1536]{4,3,1,2,0:T(8,128)(2,1)S(1)} all-to-all(bf16[2,8,1,48,1536]{4,3,1,2,0:T(8,128)(2,1)S(1)} %pad_maximum_fusion), channel_id=1, replica_groups=mesh['groups'=2,'expert'=2,'tensor'=8] {'expert'}, dimensions={0} | all-to-all | bytes 4718592 | tf_op jit(solution)/shard_map/all_to_all | solution.py:54
  124.6 0.2 copy.39
  124.8 1.8 convolution_convert_fusion.2
  126.6 8.1 %fusion.24 = bf16[768,1536]{1,0:T(8,128)(2,1)S(1)} fusion(bf16[768,2048]{1,0:T(8,128)(2,1)S(1)} %fusion.12, bf16[1,2048,3072]{2,1,0:T(8,128)(2,1)} %param.11), kind=kOutput, calls=%fused_computation.22 | convolution fusion | flops 4833017856 | bytes 11796480 | tf_op jit(solution)/shard_map/dot_general | solution.py:51
  134.7 0.2 slice_bitcast_fusion.1
  134.9 0.2 pad_maximum_fusion.1
  135.1 5.6 %all_to_all.17 = bf16[2,8,1,48,1536]{4,3,1,2,0:T(8,128)(2,1)S(1)} all-to-all(bf16[2,8,1,48,1536]{4,3,1,2,0:T(8,128)(2,1)S(1)} %pad_maximum_fusion.1), channel_id=1, replica_groups=mesh['groups'=2,'expert'=2,'tensor'=8] {'expert'}, dimensions={0} | all-to-all | bytes 4718592 | tf_op jit(solution)/shard_map/all_to_all | solution.py:54
  140.7 0.2 copy.41
  140.9 1.8 convolution_convert_fusion.1
  142.7 48.2 %reduce-scatter.3.cloned.1.call-done = bf16[64,1536]{1,0:T(8,128)(2,1)} async-done(((bf16[512,1536]{1,0:T(8,128)(2,1)}), bf16[64,1536]{1,0:T(8,128)(2,1)}) %reduce-scatter.3.cloned.1.call-update) | async-done | bytes 196624 | tf_op jit(solution)/shard_map/reduce_scatter | solution.py:61
  191.0 68.0 %reduce-scatter.5.cloned.1.call-done = bf16[64,1536]{1,0:T(8,128)(2,1)} async-done(((bf16[512,1536]{1,0:T(8,128)(2,1)}), bf16[64,1536]{1,0:T(8,128)(2,1)}) %reduce-scatter.5.cloned.1.call-update) | async-done | bytes 196624 | tf_op jit(solution)/shard_map/reduce_scatter | solution.py:61
  258.9 1.2 multiply_convert_fusion.1
  260.1 0.8 pad_maximum_fusion.2
  (15 shorter events, 0.1 us)
Async XLA Ops:
  6.5 65.8 %all-gather.3.cloned.1.call-start = ((), (), s32[]{:S(2)}) async-start(), calls=%async_computation.7 | async-start | bytes 3538944 | tf_op jit(solution)/shard_map/all_gather | solution.py:36
  7.3 183.7 %reduce-scatter.3.cloned.1.call-start = ((), (), s32[]{:S(2)}) async-start(), calls=%async_computation.5 | async-start | bytes 1769472 | tf_op jit(solution)/shard_map/reduce_scatter | solution.py:61
  75.7 8.8 %slice-start = ((s8[12582912]{0:T(1024)(128)(4,1)}), s8[4194304]{0:T(1024)(128)(4,1)S(1)}, s32[]{:S(2)}) async-start(s8[12582912]{0:T(1024)(128)(4,1)} %bitcast.63), calls=%async_computation.8 | async-start | bytes 8388608
  76.1 8.4 %slice-start.1 = ((s8[12582912]{0:T(1024)(128)(4,1)}), s8[4194304]{0:T(1024)(128)(4,1)S(1)}, s32[]{:S(2)}) async-start(s8[12582912]{0:T(1024)(128)(4,1)} %bitcast.63), calls=%async_computation.9 | async-start | bytes 8388608
  84.1 2.2 slice-start.2
  126.6 132.4 %reduce-scatter.5.cloned.1.call-start = ((), (), s32[]{:S(2)}) async-start(), calls=%async_computation.6 | async-start | bytes 1769472 | tf_op jit(solution)/shard_map/reduce_scatter | solution.py:61
  140.9 118.0 %copy-start = (f32[64]{0:T(128)S(1)}, f32[64]{0:T(128)}, u32[]{:S(2)}) copy-start(f32[64]{0:T(128)} %param.8) | copy-start | bytes 772
Sparse Core Ops, SparseCore 0:
  9.5 62.7 all-gather.2
  126.7 64.2 reduce-scatter.2
  194.4 64.4 reduce-scatter.4
